TPU v7x, 32 devices: a whole 2x2x4 slice. The times are simulated.
32 devices in a mesh: row: 8 (over y, x, core), col: 4 (over z).
Axes of the slice: x: 2, y: 2, z: 4, core: 2. Of those that a mesh axis runs over, the one named last changes fastest.
Arguments:
- mode_block: float32 [32768, 256], P(('row', 'col')), may hold values from -80 to 80
- k_blocks: float32 [256, 3, 128, 128], P(('row', 'col')), may hold values from -1 to 9
- block_cols: int32 [256, 3], P(('row', 'col')), may hold values from 0 to 255, as said below
- panel_node: int32 [4096], replicated, may hold values from 0 to 32767, as said below
- added_mass: bfloat16 [4096, 4096], P('row', 'col'), may hold values from -0.125 to 0.125
- low_edge: int32 [256], replicated, may hold values from 4 to 8
- high_edge: int32 [256], replicated, may hold values from 40 to 56
Outputs:
- filtered: float32 [32768, 256], P(('row', 'col'))
Inputs may be any that keep to these rules, and one draw needn't show every extreme that they name: `panel_node`: distinct shell rows. Cut the panels into 32 aligned blocks of 128; in each block at most 8 panels lie on the 1024 rows of one shell device (rows d * 1024 to (d + 1) * 1024 - 1), exactly 8 for some device, and the panels of a block on one device are consecutive. `block_cols`: row i holds i first, then two different block rows among i - 2 to i + 2 other than i.
All inputs are finite; a program needn't handle non-finite values.
Results may differ from a plain program's by a relative error of at most 0.0015.
Values may be sent and summed in bfloat16 or wider, within the bound.
A program may use at most 64 MiB of HBM per device.

v0:
```python
import jax
import jax.numpy as jnp
from jax import lax
from jax.sharding import PartitionSpec as P

DEGREE = 3
OUTER = 2


def with_halo(block, sides, width):
    for axis, dim in sides:
        count = lax.axis_size(axis)
        forward = [(i, i + 1) for i in range(count - 1)]
        backward = [(target, source) for source, target in forward]
        low = lax.ppermute(
            lax.slice_in_dim(block, block.shape[dim] - width, None, axis=dim), axis, forward
        )
        high = lax.ppermute(lax.slice_in_dim(block, 0, width, axis=dim), axis, backward)
        block = jnp.concatenate([low, block, high], axis=dim)
    return block


def body(mode_block, k_blocks, block_cols, panel_node, added_mass, low_edge, high_edge):
    n_row = lax.axis_size("row")
    n_col = lax.axis_size("col")
    devices = n_row * n_col
    my_row = lax.axis_index("row")
    my_col = lax.axis_index("col")
    linear = my_row * n_col + my_col
    rows_dev = mode_block.shape[0]
    mode_width = mode_block.shape[1]
    block_size = k_blocks.shape[2]
    blocks_dev = rows_dev // block_size
    panel_count = panel_node.shape[0]
    per_block = panel_count // devices
    slot_count = 2 * ((per_block + devices - 1) // devices)
    flat_total = devices * slot_count
    panel_rows = panel_node.reshape(devices, per_block)
    source = panel_rows // rows_dev
    within = jnp.arange(per_block)
    earlier = within[None, :] < within[:, None]
    same_source = source[:, :, None] == source[:, None, :]
    slot_rank = jnp.sum((same_source & earlier[None, :, :]).astype(jnp.int32), axis=2)
    block_ids = jnp.arange(devices)[:, None]
    target = block_ids % n_row * n_col + block_ids // n_row
    owned = source == linear
    local_row = panel_rows - linear * rows_dev
    send_flat = jnp.where(owned, target * slot_count + slot_rank, flat_total)
    send_index = jnp.full((flat_total,), rows_dev, dtype=jnp.int32)
    send_index = send_index.at[send_flat.reshape(-1)].set(local_row.reshape(-1), mode="drop")
    return_rows = jnp.where(owned, local_row, rows_dev)
    return_index = jnp.full((rows_dev,), flat_total, dtype=jnp.int32)
    return_index = return_index.at[return_rows.reshape(-1)].set(
        (block_ids * slot_count + slot_rank).reshape(-1), mode="drop"
    )
    in_block = my_col * n_row + my_row
    in_source = lax.dynamic_index_in_dim(source, in_block, 0, keepdims=False)
    in_slot = lax.dynamic_index_in_dim(slot_rank, in_block, 0, keepdims=False)
    in_flat = in_source * slot_count + in_slot
    out_source = lax.dynamic_index_in_dim(source, linear, 0, keepdims=False)
    out_slot = lax.dynamic_index_in_dim(slot_rank, linear, 0, keepdims=False)
    out_index = jnp.full((flat_total,), per_block, dtype=jnp.int32)
    out_index = out_index.at[out_source * slot_count + out_slot].set(within)
    row_source = lax.dynamic_slice_in_dim(source, my_row * n_col, n_col, 0)
    row_slot = lax.dynamic_slice_in_dim(slot_rank, my_row * n_col, n_col, 0)
    row_flat = (
        row_source * (n_col * slot_count) + jnp.arange(n_col)[:, None] * slot_count + row_slot
    )
    part_index = jnp.full((devices * n_col * slot_count,), n_col * per_block, dtype=jnp.int32)
    part_index = part_index.at[row_flat.reshape(-1)].set(jnp.arange(n_col * per_block))
    local_cols = block_cols - (linear * blocks_dev - 2)
    zero_bf = jnp.zeros((1, mode_width), jnp.bfloat16)
    zero_row = jnp.zeros((1, mode_width), jnp.float32)

    def stiffness(vectors):
        padded = with_halo(vectors, ((("row", "col"), 0),), 2 * block_size)
        pieces = padded.reshape(blocks_dev + 4, block_size, mode_width)
        chosen = pieces[local_cols]
        product = jnp.einsum("rkij,rkjn->rin", k_blocks, chosen, precision=lax.Precision.HIGHEST)
        return product.reshape(rows_dev, mode_width)

    def accumulate(arrived_piece):
        return jnp.dot(added_mass, arrived_piece, preferred_element_type=jnp.float32)

    def fluid_loads(vectors):
        rounded = jnp.concatenate([vectors.astype(jnp.bfloat16), zero_bf], axis=0)
        outgoing = rounded[send_index]
        arrived = lax.all_to_all(
            outgoing.reshape(devices, slot_count, mode_width),
            ("row", "col"),
            split_axis=0,
            concat_axis=0,
            tiled=True,
        )
        arrived = arrived.reshape(flat_total, mode_width)
        wetted = arrived[in_flat]
        partial_value = accumulate(lax.all_gather(wetted, "row", axis=0, tiled=True))
        pressure = lax.psum_scatter(partial_value, "col", scatter_dimension=0, tiled=True)
        padded_press = jnp.concatenate([pressure, zero_row], axis=0)
        sending = padded_press[out_index].reshape(devices, slot_count, mode_width)
        summed = lax.all_to_all(
            sending, ("row", "col"), split_axis=0, concat_axis=0, tiled=True
        ).reshape(flat_total, mode_width)
        padded_sum = jnp.concatenate([summed, zero_row], axis=0)
        return padded_sum[return_index]

    def operate(vectors):
        return stiffness(vectors) + fluid_loads(vectors)

    lower = low_edge.astype(jnp.float32) * 0.25
    upper = high_edge.astype(jnp.float32) * 0.25
    centre = 0.5 * (upper + lower)
    radius = 0.5 * (upper - lower)
    total_rows = rows_dev * devices
    current = mode_block
    for outer_no in range(OUTER):
        previous = current
        current = (operate(current) - centre * current) / radius
        for degree_no in range(DEGREE - 1):
            following = 2.0 * (operate(current) - centre * current) / radius - previous
            previous = current
            current = following
        squares = lax.psum(jnp.sum(current * current, axis=0), ("row", "col"))
        current = current / jnp.sqrt(squares / total_rows + 1e-06)
    return current


def solution(mesh):
    placed = (
        P(("row", "col"), None),
        P(("row", "col"), None, None, None),
        P(("row", "col"), None),
        P(),
        P("row", "col"),
        P(),
        P(),
    )
    return jax.shard_map(
        body, mesh=mesh, in_specs=placed, out_specs=P(("row", "col"), None), check_vma=False
    )
```

profile of v0, /device:TPU:0, one launch (start us, length us, event | category | flops | bytes accessed | tf_op | source)
XLA Modules:
  0.0 587.2 jit_solution(11731140511086322295)
XLA Ops:
  9.5 15.5 %scatter_custom_fusion = s32[256]{0:T(256)S(1)} fusion(s32[4096]{0:T(1024)S(1)} %get-tuple-element.35, s32[4096]{0:T(1024)S(1)} %get-tuple-element.20, s32[]{:T(128)} %constant.94.clone.1), kind=kCustom, calls=%fused_computation.139 | custom fusion | bytes 1028 | tf_op jit(solution)/shard_map/scatter | solution.py:50
  28.2 7.3 %all-to-all-start = ((bf16[32,8,256]{2,1,0:T(8,128)(2,1)}), bf16[32,8,256]{2,1,0:T(8,128)(2,1)S(1)}, u32[]{:S(2)}, u32[]{:S(2)}) async-start(bf16[32,8,256]{2,1,0:T(8,128)(2,1)} %bitcast.8), calls=%async_computation | async-start | bytes 262144 | tf_op jit(solution)/shard_map/all_to_all | solution.py:88
  37.4 3.7 collective-permute-start
  44.8 13.9 %all-gather = bf16[1024,256]{1,0:T(8,128)(2,1)S(1)} all-gather(bf16[128,256]{1,0:T(8,128)(2,1)S(1)} %gather_fusion.2), channel_id=2, replica_groups=mesh['row'=8,'col'=4] {'row'}, dimensions={0}, use_global_device_ids=true | all-gather | bytes 589824 | tf_op jit(solution)/shard_map/all_gather | solution.py:97
  60.3 15.5 %scatter_custom_fusion.2 = s32[1024]{0:T(1024)S(1)} fusion(s32[4096]{0:T(1024)S(1)} %get-tuple-element.19, s32[4096]{0:T(1024)S(1)} %add_bitcast_fusion, s32[]{:T(128)} %constant.101.clone.1), kind=kCustom, calls=%fused_computation.110 | custom fusion | bytes 4100 | tf_op jit(solution)/shard_map/scatter | solution.py:53
  75.8 4.1 reduce-scatter.7.cloned.1.call-done
  82.6 2.9 all-to-all-start.1
  85.5 2.6 pad_maximum_fusion
  88.1 3.8 gather_fusion
  91.9 5.1 fusion.59
  97.1 4.7 gather_fusion.4
  101.8 3.0 fusion.51
  106.0 14.0 %all_to_all.60 = bf16[32,8,256]{2,1,0:T(8,128)(2,1)S(1)} all-to-all(bf16[32,8,256]{2,1,0:T(8,128)(2,1)S(1)} %bitcast.215), channel_id=1, replica_groups=mesh['row'=8,'col'=4] {'row','col'}, dimensions={0} | all-to-all | bytes 262144 | tf_op jit(solution)/shard_map/all_to_all | solution.py:88
  120.8 9.6 %all-gather.1 = bf16[1024,256]{1,0:T(8,128)(2,1)S(1)} all-gather(bf16[128,256]{1,0:T(8,128)(2,1)S(1)} %gather_fusion.7), channel_id=3, replica_groups=mesh['row'=8,'col'=4] {'row'}, dimensions={0}, use_global_device_ids=true | all-gather | bytes 589824 | tf_op jit(solution)/shard_map/all_gather | solution.py:97
  131.7 1.9 fusion.57
  136.7 20.1 %reduce-scatter.9.cloned.1.call-done = f32[128,256]{0,1:T(8,128)} async-done(((f32[512,256]{0,1:T(8,128)}), f32[128,256]{0,1:T(8,128)}) %reduce-scatter.9.cloned.1.call-update) | async-done | bytes 131088 | tf_op jit(solution)/shard_map/reduce_scatter | solution.py:98
  159.5 4.7 all-to-all-start.3
  164.2 2.6 pad_maximum_fusion.1
  166.8 3.8 gather_fusion.5
  170.6 5.1 fusion.60
  175.8 4.7 gather_fusion.9
  180.5 3.4 fusion.49
  185.1 14.0 %all_to_all.61 = bf16[32,8,256]{2,1,0:T(8,128)(2,1)S(1)} all-to-all(bf16[32,8,256]{2,1,0:T(8,128)(2,1)S(1)} %bitcast.216), channel_id=1, replica_groups=mesh['row'=8,'col'=4] {'row','col'}, dimensions={0} | all-to-all | bytes 262144 | tf_op jit(solution)/shard_map/all_to_all | solution.py:88
  200.0 9.1 %all-gather.2 = bf16[1024,256]{1,0:T(8,128)(2,1)S(1)} all-gather(bf16[128,256]{1,0:T(8,128)(2,1)S(1)} %gather_fusion.12), channel_id=4, replica_groups=mesh['row'=8,'col'=4] {'row'}, dimensions={0}, use_global_device_ids=true | all-gather | bytes 589824 | tf_op jit(solution)/shard_map/all_gather | solution.py:97
  210.4 1.9 fusion.56
  215.4 20.1 %reduce-scatter.11.cloned.1.call-done = f32[128,256]{0,1:T(8,128)} async-done(((f32[512,256]{0,1:T(8,128)}), f32[128,256]{0,1:T(8,128)}) %reduce-scatter.11.cloned.1.call-update) | async-done | bytes 131088 | tf_op jit(solution)/shard_map/reduce_scatter | solution.py:98
  238.2 4.6 all-to-all-start.5
  243.0 2.6 pad_maximum_fusion.2
  245.6 3.8 gather_fusion.10
  249.4 5.1 fusion.61
  254.6 4.7 gather_fusion.14
  259.3 3.4 multiply_reduce_fusion.1
  262.7 40.4 %psum.14 = f32[256]{0:T(256)S(1)} all-reduce(f32[256]{0:T(256)S(1)} %get-tuple-element.13), channel_id=1, replica_groups=mesh['row'=8,'col'=4] {'row','col'}, use_global_device_ids=true, to_apply=%region_8.9 | all-reduce | flops 256 | bytes 2048 | tf_op jit(solution)/shard_map/psum | solution.py:123
  303.1 2.3 fusion.47
  306.6 12.7 %all_to_all.62 = bf16[32,8,256]{2,1,0:T(8,128)(2,1)S(1)} all-to-all(bf16[32,8,256]{2,1,0:T(8,128)(2,1)S(1)} %bitcast.217), channel_id=1, replica_groups=mesh['row'=8,'col'=4] {'row','col'}, dimensions={0} | all-to-all | bytes 262144 | tf_op jit(solution)/shard_map/all_to_all | solution.py:88
  320.1 9.1 %all-gather.3 = bf16[1024,256]{1,0:T(8,128)(2,1)S(1)} all-gather(bf16[128,256]{1,0:T(8,128)(2,1)S(1)} %gather_fusion.17), channel_id=5, replica_groups=mesh['row'=8,'col'=4] {'row'}, dimensions={0}, use_global_device_ids=true | all-gather | bytes 589824 | tf_op jit(solution)/shard_map/all_gather | solution.py:97
  330.6 1.9 fusion.55
  335.5 20.1 %reduce-scatter.13.cloned.1.call-done = f32[128,256]{0,1:T(8,128)} async-done(((f32[512,256]{0,1:T(8,128)}), f32[128,256]{0,1:T(8,128)}) %reduce-scatter.13.cloned.1.call-update) | async-done | bytes 131088 | tf_op jit(solution)/shard_map/reduce_scatter | solution.py:98
  358.3 4.6 all-to-all-start.7
  363.0 2.6 pad_maximum_fusion.3
  365.6 3.8 gather_fusion.15
  369.4 5.1 fusion.62
  374.5 4.7 gather_fusion.19
  379.3 3.1 fusion.45
  383.5 14.0 %all_to_all.63 = bf16[32,8,256]{2,1,0:T(8,128)(2,1)S(1)} all-to-all(bf16[32,8,256]{2,1,0:T(8,128)(2,1)S(1)} %bitcast.218), channel_id=1, replica_groups=mesh['row'=8,'col'=4] {'row','col'}, dimensions={0} | all-to-all | bytes 262144 | tf_op jit(solution)/shard_map/all_to_all | solution.py:88
  398.4 9.3 %all-gather.4 = bf16[1024,256]{1,0:T(8,128)(2,1)S(1)} all-gather(bf16[128,256]{1,0:T(8,128)(2,1)S(1)} %gather_fusion.22), channel_id=6, replica_groups=mesh['row'=8,'col'=4] {'row'}, dimensions={0}, use_global_device_ids=true | all-gather | bytes 589824 | tf_op jit(solution)/shard_map/all_gather | solution.py:97
  409.0 1.9 fusion.54
  414.0 20.1 %reduce-scatter.15.cloned.1.call-done = f32[128,256]{0,1:T(8,128)} async-done(((f32[512,256]{0,1:T(8,128)}), f32[128,256]{0,1:T(8,128)}) %reduce-scatter.15.cloned.1.call-update) | async-done | bytes 131088 | tf_op jit(solution)/shard_map/reduce_scatter | solution.py:98
  436.7 4.6 all-to-all-start.9
  441.5 2.6 pad_maximum_fusion.4
  444.1 3.8 gather_fusion.20
  447.8 5.1 fusion.63
  453.0 4.7 gather_fusion.24
  457.7 3.4 fusion.43
  462.3 14.0 %all_to_all.64 = bf16[32,8,256]{2,1,0:T(8,128)(2,1)S(1)} all-to-all(bf16[32,8,256]{2,1,0:T(8,128)(2,1)S(1)} %bitcast.214), channel_id=1, replica_groups=mesh['row'=8,'col'=4] {'row','col'}, dimensions={0} | all-to-all | bytes 262144 | tf_op jit(solution)/shard_map/all_to_all | solution.py:88
  477.2 9.1 %all-gather.5 = bf16[1024,256]{1,0:T(8,128)(2,1)S(1)} all-gather(bf16[128,256]{1,0:T(8,128)(2,1)S(1)} %gather_fusion.27), channel_id=7, replica_groups=mesh['row'=8,'col'=4] {'row'}, dimensions={0}, use_global_device_ids=true | all-gather | bytes 589824 | tf_op jit(solution)/shard_map/all_gather | solution.py:97
  491.8 21.1 %reduce-scatter.17.cloned.1.call-done = f32[128,256]{0,1:T(8,128)} async-done(((f32[512,256]{0,1:T(8,128)}), f32[128,256]{0,1:T(8,128)}) %reduce-scatter.17.cloned.1.call-update) | async-done | bytes 131088 | tf_op jit(solution)/shard_map/reduce_scatter | solution.py:98
  515.5 4.3 all-to-all-start.11
  519.8 2.5 pad_maximum_fusion.5
  522.3 3.8 gather_fusion.25
  526.1 5.1 fusion.64
  531.3 4.7 gather_fusion.29
  536.0 2.5 multiply_reduce_fusion
  538.5 40.5 %psum.15 = f32[256]{0:T(256)S(1)} all-reduce(f32[256]{0:T(256)S(1)} %get-tuple-element.5), channel_id=1, replica_groups=mesh['row'=8,'col'=4] {'row','col'}, use_global_device_ids=true, to_apply=%region_13.14 | all-reduce | flops 256 | bytes 2048 | tf_op jit(solution)/shard_map/psum | solution.py:123
  (127 shorter events, 63.8 us)
Async XLA Ops:
  6.5 85.4 %copy-start = (f32[8,3,128,128]{3,2,1,0:T(8,128)S(1)}, f32[8,3,128,128]{3,2,1,0:T(8,128)}, u32[]{:S(2)}) copy-start(f32[8,3,128,128]{3,2,1,0:T(8,128)} %param.8) | copy-start | bytes 4718596
  26.3 17.1 %copy-start.2 = (s32[8,3]{0,1:T(4,128)S(1)}, s32[8,3]{0,1:T(4,128)}, u32[]{:S(2)}) copy-start(s32[8,3]{0,1:T(4,128)} %param.9) | copy-start | bytes 292
  26.4 32.3 %copy-start.1 = (bf16[512,1024]{1,0:T(8,128)(2,1)S(1)}, bf16[512,1024]{1,0:T(8,128)(2,1)}, u32[]{:S(2)}) copy-start(bf16[512,1024]{1,0:T(8,128)(2,1)} %param.11) | copy-start | bytes 3145732
  28.2 15.7 %all-to-all-start = ((bf16[32,8,256]{2,1,0:T(8,128)(2,1)}), bf16[32,8,256]{2,1,0:T(8,128)(2,1)S(1)}, u32[]{:S(2)}, u32[]{:S(2)}) async-start(bf16[32,8,256]{2,1,0:T(8,128)(2,1)} %bitcast.8), calls=%async_computation | async-start | bytes 262144 | tf_op jit(solution)/shard_map/all_to_all | solution.py:88
  35.5 44.4 %reduce-scatter.7.cloned.1.call-start = ((), (), s32[]{:S(2)}) async-start(), calls=%async_computation.18 | async-start | bytes 655360 | tf_op jit(solution)/shard_map/reduce_scatter | solution.py:98
  37.4 48.1 %collective-permute-start = (f32[256,256]{1,0:T(8,128)}, f32[256,256]{1,0:T(8,128)S(1)}, u32[]{:S(2)}, u32[]{:S(2)}) collective-permute-start(f32[256,256]{1,0:T(8,128)} %get-tuple-element.31), channel_id=1, source_target_pairs={{0,1},{1,2},{2,3},{3,4},{4,5},{5,6},{6,7},{7,8},{8,9},{9,10},{10,1... | collective-permute-start | bytes 786440 | tf_op jit(solution)/shard_map/ppermute | solution.py:15
  41.1 44.4 %collective-permute-start.1 = (f32[256,256]{1,0:T(8,128)}, f32[256,256]{1,0:T(8,128)}, u32[]{:S(2)}, u32[]{:S(2)}) collective-permute-start(f32[256,256]{1,0:T(8,128)} %get-tuple-element.32), channel_id=1, source_target_pairs={{1,0},{2,1},{3,2},{4,3},{5,4},{6,5},{7,6},{8,7},{9,8},{10,9},{11,1... | collective-permute-start | bytes 786440 | tf_op jit(solution)/shard_map/ppermute | solution.py:18
  44.8 15.4 %copy-start.3 = (s32[256]{0:T(256)S(1)}, s32[256]{0:T(256)}, u32[]{:S(2)}) copy-start(s32[256]{0:T(256)} %param.13) | copy-start | bytes 3076
  44.8 15.4 %copy-start.4 = (s32[256]{0:T(256)S(1)}, s32[256]{0:T(256)}, u32[]{:S(2)}) copy-start(s32[256]{0:T(256)} %param.12) | copy-start | bytes 3076
  82.6 14.5 %all-to-all-start.1 = ((f32[32,8,256]{2,1,0:T(8,128)}), f32[32,8,256]{2,1,0:T(8,128)S(1)}, u32[]{:S(2)}, u32[]{:S(2)}) async-start(f32[32,8,256]{2,1,0:T(8,128)} %bitcast.15), calls=%async_computation.2 | async-start | bytes 524288 | tf_op jit(solution)/shard_map/all_to_all | solution.py:101
  85.5 71.3 %reduce-scatter.9.cloned.1.call-start = ((), (), s32[]{:S(2)}) async-start(), calls=%async_computation.19 | async-start | bytes 655360 | tf_op jit(solution)/shard_map/reduce_scatter | solution.py:98
  133.6 30.5 %collective-permute-start.2 = (f32[256,256]{1,0:T(8,128)}, f32[256,256]{1,0:T(8,128)S(1)}, u32[]{:S(2)}, u32[]{:S(2)}) collective-permute-start(f32[256,256]{1,0:T(8,128)} %get-tuple-element.29), channel_id=1, source_target_pairs={{0,1},{1,2},{2,3},{3,4},{4,5},{5,6},{6,7},{7,8},{8,9},{9,10},{10,1... | collective-permute-start | bytes 786440 | tf_op jit(solution)/shard_map/ppermute | solution.py:15
  135.4 28.8 %collective-permute-start.3 = (f32[256,256]{1,0:T(8,128)}, f32[256,256]{1,0:T(8,128)}, u32[]{:S(2)}, u32[]{:S(2)}) collective-permute-start(f32[256,256]{1,0:T(8,128)} %get-tuple-element.30), channel_id=1, source_target_pairs={{1,0},{2,1},{3,2},{4,3},{5,4},{6,5},{7,6},{8,7},{9,8},{10,9},{11,1... | collective-permute-start | bytes 786440 | tf_op jit(solution)/shard_map/ppermute | solution.py:18
  159.5 16.3 %all-to-all-start.3 = ((f32[32,8,256]{2,1,0:T(8,128)}), f32[32,8,256]{2,1,0:T(8,128)S(1)}, u32[]{:S(2)}, u32[]{:S(2)}) async-start(f32[32,8,256]{2,1,0:T(8,128)} %bitcast.27), calls=%async_computation.5 | async-start | bytes 524288 | tf_op jit(solution)/shard_map/all_to_all | solution.py:101
  164.1 71.3 %reduce-scatter.11.cloned.1.call-start = ((), (), s32[]{:S(2)}) async-start(), calls=%async_computation.20 | async-start | bytes 655360 | tf_op jit(solution)/shard_map/reduce_scatter | solution.py:98
  212.3 30.7 %collective-permute-start.4 = (f32[256,256]{1,0:T(8,128)}, f32[256,256]{1,0:T(8,128)S(1)}, u32[]{:S(2)}, u32[]{:S(2)}) collective-permute-start(f32[256,256]{1,0:T(8,128)} %get-tuple-element.27), channel_id=1, source_target_pairs={{0,1},{1,2},{2,3},{3,4},{4,5},{5,6},{6,7},{7,8},{8,9},{9,10},{10,1... | collective-permute-start | bytes 786440 | tf_op jit(solution)/shard_map/ppermute | solution.py:15
  214.1 28.9 %collective-permute-start.5 = (f32[256,256]{1,0:T(8,128)}, f32[256,256]{1,0:T(8,128)}, u32[]{:S(2)}, u32[]{:S(2)}) collective-permute-start(f32[256,256]{1,0:T(8,128)} %get-tuple-element.28), channel_id=1, source_target_pairs={{1,0},{2,1},{3,2},{4,3},{5,4},{6,5},{7,6},{8,7},{9,8},{10,9},{11,1... | collective-permute-start | bytes 786440 | tf_op jit(solution)/shard_map/ppermute | solution.py:18
  238.2 16.4 %all-to-all-start.5 = ((f32[32,8,256]{2,1,0:T(8,128)}), f32[32,8,256]{2,1,0:T(8,128)S(1)}, u32[]{:S(2)}, u32[]{:S(2)}) async-start(f32[32,8,256]{2,1,0:T(8,128)} %bitcast.38), calls=%async_computation.8 | async-start | bytes 524288 | tf_op jit(solution)/shard_map/all_to_all | solution.py:101
  242.8 112.8 %reduce-scatter.13.cloned.1.call-start = ((), (), s32[]{:S(2)}) async-start(), calls=%async_computation.21 | async-start | bytes 655360 | tf_op jit(solution)/shard_map/reduce_scatter | solution.py:98
  332.5 30.5 %collective-permute-start.6 = (f32[256,256]{1,0:T(8,128)}, f32[256,256]{1,0:T(8,128)S(1)}, u32[]{:S(2)}, u32[]{:S(2)}) collective-permute-start(f32[256,256]{1,0:T(8,128)} %get-tuple-element.25), channel_id=1, source_target_pairs={{0,1},{1,2},{2,3},{3,4},{4,5},{5,6},{6,7},{7,8},{8,9},{9,10},{10,1... | collective-permute-start | bytes 786440 | tf_op jit(solution)/shard_map/ppermute | solution.py:15
  334.2 28.8 %collective-permute-start.7 = (f32[256,256]{1,0:T(8,128)}, f32[256,256]{1,0:T(8,128)}, u32[]{:S(2)}, u32[]{:S(2)}) collective-permute-start(f32[256,256]{1,0:T(8,128)} %get-tuple-element.26), channel_id=1, source_target_pairs={{1,0},{2,1},{3,2},{4,3},{5,4},{6,5},{7,6},{8,7},{9,8},{10,9},{11,1... | collective-permute-start | bytes 786440 | tf_op jit(solution)/shard_map/ppermute | solution.py:18
  358.3 16.2 %all-to-all-start.7 = ((f32[32,8,256]{2,1,0:T(8,128)}), f32[32,8,256]{2,1,0:T(8,128)S(1)}, u32[]{:S(2)}, u32[]{:S(2)}) async-start(f32[32,8,256]{2,1,0:T(8,128)} %bitcast.49), calls=%async_computation.11 | async-start | bytes 524288 | tf_op jit(solution)/shard_map/all_to_all | solution.py:101
  362.9 71.1 %reduce-scatter.15.cloned.1.call-start = ((), (), s32[]{:S(2)}) async-start(), calls=%async_computation.22 | async-start | bytes 655360 | tf_op jit(solution)/shard_map/reduce_scatter | solution.py:98
  410.9 30.5 %collective-permute-start.8 = (f32[256,256]{1,0:T(8,128)}, f32[256,256]{1,0:T(8,128)S(1)}, u32[]{:S(2)}, u32[]{:S(2)}) collective-permute-start(f32[256,256]{1,0:T(8,128)} %get-tuple-element.23), channel_id=1, source_target_pairs={{0,1},{1,2},{2,3},{3,4},{4,5},{5,6},{6,7},{7,8},{8,9},{9,10},{10,1... | collective-permute-start | bytes 786440 | tf_op jit(solution)/shard_map/ppermute | solution.py:15
  412.7 28.7 %collective-permute-start.9 = (f32[256,256]{1,0:T(8,128)}, f32[256,256]{1,0:T(8,128)}, u32[]{:S(2)}, u32[]{:S(2)}) collective-permute-start(f32[256,256]{1,0:T(8,128)} %get-tuple-element.24), channel_id=1, source_target_pairs={{1,0},{2,1},{3,2},{4,3},{5,4},{6,5},{7,6},{8,7},{9,8},{10,9},{11,1... | collective-permute-start | bytes 786440 | tf_op jit(solution)/shard_map/ppermute | solution.py:18
  436.7 16.2 %all-to-all-start.9 = ((f32[32,8,256]{2,1,0:T(8,128)}), f32[32,8,256]{2,1,0:T(8,128)S(1)}, u32[]{:S(2)}, u32[]{:S(2)}) async-start(f32[32,8,256]{2,1,0:T(8,128)} %bitcast.60), calls=%async_computation.14 | async-start | bytes 524288 | tf_op jit(solution)/shard_map/all_to_all | solution.py:101
  441.4 71.5 %reduce-scatter.17.cloned.1.call-start = ((), (), s32[]{:S(2)}) async-start(), calls=%async_computation.23 | async-start | bytes 655360 | tf_op jit(solution)/shard_map/reduce_scatter | solution.py:98
  488.7 31.2 %collective-permute-start.10 = (f32[256,256]{1,0:T(8,128)S(1)}, f32[256,256]{1,0:T(8,128)S(1)}, u32[]{:S(2)}, u32[]{:S(2)}) collective-permute-start(f32[256,256]{1,0:T(8,128)S(1)} %get-tuple-element.21), channel_id=1, source_target_pairs={{0,1},{1,2},{2,3},{3,4},{4,5},{5,6},{6,7},{7,8},{8,9},{9,10},{10,1... | collective-permute-start | bytes 786440 | tf_op jit(solution)/shard_map/ppermute | solution.py:15
  490.5 29.4 %collective-permute-start.11 = (f32[256,256]{1,0:T(8,128)S(1)}, f32[256,256]{1,0:T(8,128)S(1)}, u32[]{:S(2)}, u32[]{:S(2)}) collective-permute-start(f32[256,256]{1,0:T(8,128)S(1)} %get-tuple-element.22), channel_id=1, source_target_pairs={{1,0},{2,1},{3,2},{4,3},{5,4},{6,5},{7,6},{8,7},{9,8},{10,9},{11,1... | collective-permute-start | bytes 786440 | tf_op jit(solution)/shard_map/ppermute | solution.py:18
  515.5 15.7 %all-to-all-start.11 = ((f32[32,8,256]{2,1,0:T(8,128)}), f32[32,8,256]{2,1,0:T(8,128)S(1)}, u32[]{:S(2)}, u32[]{:S(2)}) async-start(f32[32,8,256]{2,1,0:T(8,128)} %bitcast.71), calls=%async_computation.17 | async-start | bytes 524288 | tf_op jit(solution)/shard_map/all_to_all | solution.py:101
Sparse Core Ops, SparseCore 0:
  60.1 19.7 reduce-scatter.6
  131.9 24.8 reduce-scatter.8
  210.5 24.8 reduce-scatter.10
  330.7 24.8 reduce-scatter.12
  409.1 24.8 reduce-scatter.14
  487.7 25.0 reduce-scatter.16
where the time goes:
time: 597 us; the launch traced here: 587 us
  blocking collectives  210 us (35%)
  local copies, waits for them, and re-layouts  123 us (21%)
  waiting for transfers between devices  106 us (18%)
  starting transfers between devices  53.7 us (9%)
  other arithmetic  42.1 us (7%)
  matrix products  38.6 us (6%)
  between operations  14.5 us (2%)
    reduce_scatter x6, waiting for transfers between devices, fluid_loads(): lax.psum_scatter(partial_value, 'col', scatter_dimension=0, tiled=True)  105 us
    psum x2, blocking collectives, body(): squares = lax.psum(jnp.sum(current * current, axis=0), ('row', 'col'))  80.9 us
    all_to_all x5, blocking collectives, fluid_loads(): lax.all_to_all(outgoing.reshape(devices, slot_count, mode_width), ('row',...  68.7 us
    all_gather x6, blocking collectives, fluid_loads(): lax.all_gather(wetted, 'row', axis=0, tiled=True)  60.2 us
    dot_general x6, matrix products, stiffness(): jnp.einsum('rkij,rkjn->rin', k_blocks, chosen, precision=lax.Precision.HI...  30.9 us
    gather x6, local copies, waits for them, and re-layouts, fluid_loads(): return padded_sum[return_index]  28.2 us
    all_to_all x6, starting transfers between devices, fluid_loads(): lax.all_to_all(sending, ('row', 'col'), split_axis=0, concat_axis=0, tile...  25.7 us
    gather x6, local copies, waits for them, and re-layouts, stiffness(): chosen = pieces[local_cols]  22.7 us
  transfers between devices with their start and end apart: 25, of which 7 were waited for; matrix products, arithmetic and copies ran while one was open for 20% of the time, Pallas kernels for 0%

commit v1 on v0

--- a/solution.py
+++ b/solution.py
@@ -120,7 +120,9 @@
             following = 2.0 * (operate(current) - centre * current) / radius - previous
             previous = current
             current = following
-        squares = lax.psum(jnp.sum(current * current, axis=0), ("row", "col"))
+        squares = jnp.sum(
+            lax.all_gather(jnp.sum(current * current, axis=0), ("row", "col")), axis=0
+        )
         current = current / jnp.sqrt(squares / total_rows + 1e-06)
     return current
 

time: 597 us -> 651 us (1.090)
  blocking collectives: 210 us -> 264 us
    all_gather x0 -> x2, blocking collectives: none -> 138 us  [body(): lax.all_gather(jnp.sum(current * current, axis=0), ('row', 'col'))]
    psum x2 -> x0, blocking collectives: 80.9 us -> none  [body(): squares = lax.psum(jnp.sum(current * current, axis=0), ('row', 'col'))]
  transfers between devices with their start and end apart: 25 -> 25, of which waited for: 7 -> 7; matrix products, arithmetic and copies ran while one was open for 20% -> 18% of each run, Pallas kernels for 0% -> 0%
where the time goes in v1:
time: 651 us; the launch traced here: 641 us
  blocking collectives  264 us (41%)
  local copies, waits for them, and re-layouts  123 us (19%)
  waiting for transfers between devices  106 us (16%)
  starting transfers between devices  53.7 us (8%)
  other arithmetic  42.2 us (6%)
  matrix products  38.6 us (6%)
  between operations  14.4 us (2%)
    all_gather x2, blocking collectives, body(): lax.all_gather(jnp.sum(current * current, axis=0), ('row', 'col'))  138 us
    reduce_scatter x6, waiting for transfers between devices, fluid_loads(): lax.psum_scatter(partial_value, 'col', scatter_dimension=0, tiled=True)  105 us
    all_to_all x5, blocking collectives, fluid_loads(): lax.all_to_all(outgoing.reshape(devices, slot_count, mode_width), ('row',...  66.2 us
    all_gather x6, blocking collectives, fluid_loads(): lax.all_gather(wetted, 'row', axis=0, tiled=True)  59.9 us
    dot_general x6, matrix products, stiffness(): jnp.einsum('rkij,rkjn->rin', k_blocks, chosen, precision=lax.Precision.HI...  30.9 us
    gather x6, local copies, waits for them, and re-layouts, fluid_loads(): return padded_sum[return_index]  28.2 us
    all_to_all x6, starting transfers between devices, fluid_loads(): lax.all_to_all(sending, ('row', 'col'), split_axis=0, concat_axis=0, tile...  25.6 us
    gather x6, local copies, waits for them, and re-layouts, stiffness(): chosen = pieces[local_cols]  22.7 us
  transfers between devices with their start and end apart: 25, of which 7 were waited for; matrix products, arithmetic and copies ran while one was open for 18% of the time, Pallas kernels for 0%

profile of v1, /device:TPU:0, one launch (start us, length us, event | category | flops | bytes accessed | tf_op | source)
XLA Modules:
  0.0 641.1 jit_solution(2524085275768204309)
XLA Ops:
  9.5 15.5 %scatter_custom_fusion = s32[256]{0:T(256)S(1)} fusion(s32[4096]{0:T(1024)S(1)} %get-tuple-element.35, s32[4096]{0:T(1024)S(1)} %get-tuple-element.20, s32[]{:T(128)} %constant.94.clone.1), kind=kCustom, calls=%fused_computation.139 | custom fusion | bytes 1028 | tf_op jit(solution)/shard_map/scatter | solution.py:50
  28.2 7.3 %all-to-all-start = ((bf16[32,8,256]{2,1,0:T(8,128)(2,1)}), bf16[32,8,256]{2,1,0:T(8,128)(2,1)S(1)}, u32[]{:S(2)}, u32[]{:S(2)}) async-start(bf16[32,8,256]{2,1,0:T(8,128)(2,1)} %bitcast.8), calls=%async_computation | async-start | bytes 262144 | tf_op jit(solution)/shard_map/all_to_all | solution.py:88
  37.4 3.7 collective-permute-start
  44.8 13.9 %all-gather = bf16[1024,256]{1,0:T(8,128)(2,1)S(1)} all-gather(bf16[128,256]{1,0:T(8,128)(2,1)S(1)} %gather_fusion.2), channel_id=2, replica_groups=mesh['row'=8,'col'=4] {'row'}, dimensions={0}, use_global_device_ids=true | all-gather | bytes 589824 | tf_op jit(solution)/shard_map/all_gather | solution.py:97
  60.3 15.5 %scatter_custom_fusion.2 = s32[1024]{0:T(1024)S(1)} fusion(s32[4096]{0:T(1024)S(1)} %get-tuple-element.19, s32[4096]{0:T(1024)S(1)} %add_bitcast_fusion, s32[]{:T(128)} %constant.101.clone.1), kind=kCustom, calls=%fused_computation.110 | custom fusion | bytes 4100 | tf_op jit(solution)/shard_map/scatter | solution.py:53
  75.8 4.1 reduce-scatter.7.cloned.1.call-done
  82.6 2.9 all-to-all-start.1
  85.5 2.6 pad_maximum_fusion
  88.1 3.8 gather_fusion
  91.9 5.1 fusion.59
  97.1 4.7 gather_fusion.4
  101.8 3.0 fusion.51
  106.0 14.0 %all_to_all.60 = bf16[32,8,256]{2,1,0:T(8,128)(2,1)S(1)} all-to-all(bf16[32,8,256]{2,1,0:T(8,128)(2,1)S(1)} %bitcast.217), channel_id=1, replica_groups=mesh['row'=8,'col'=4] {'row','col'}, dimensions={0} | all-to-all | bytes 262144 | tf_op jit(solution)/shard_map/all_to_all | solution.py:88
  120.8 9.6 %all-gather.1 = bf16[1024,256]{1,0:T(8,128)(2,1)S(1)} all-gather(bf16[128,256]{1,0:T(8,128)(2,1)S(1)} %gather_fusion.7), channel_id=3, replica_groups=mesh['row'=8,'col'=4] {'row'}, dimensions={0}, use_global_device_ids=true | all-gather | bytes 589824 | tf_op jit(solution)/shard_map/all_gather | solution.py:97
  131.7 1.9 fusion.57
  136.7 20.1 %reduce-scatter.9.cloned.1.call-done = f32[128,256]{0,1:T(8,128)} async-done(((f32[512,256]{0,1:T(8,128)}), f32[128,256]{0,1:T(8,128)}) %reduce-scatter.9.cloned.1.call-update) | async-done | bytes 131088 | tf_op jit(solution)/shard_map/reduce_scatter | solution.py:98
  159.5 4.7 all-to-all-start.3
  164.2 2.6 pad_maximum_fusion.1
  166.8 3.8 gather_fusion.5
  170.6 5.1 fusion.60
  175.8 4.7 gather_fusion.9
  180.5 3.4 fusion.49
  185.1 14.0 %all_to_all.61 = bf16[32,8,256]{2,1,0:T(8,128)(2,1)S(1)} all-to-all(bf16[32,8,256]{2,1,0:T(8,128)(2,1)S(1)} %bitcast.218), channel_id=1, replica_groups=mesh['row'=8,'col'=4] {'row','col'}, dimensions={0} | all-to-all | bytes 262144 | tf_op jit(solution)/shard_map/all_to_all | solution.py:88
  200.0 9.1 %all-gather.2 = bf16[1024,256]{1,0:T(8,128)(2,1)S(1)} all-gather(bf16[128,256]{1,0:T(8,128)(2,1)S(1)} %gather_fusion.12), channel_id=4, replica_groups=mesh['row'=8,'col'=4] {'row'}, dimensions={0}, use_global_device_ids=true | all-gather | bytes 589824 | tf_op jit(solution)/shard_map/all_gather | solution.py:97
  210.4 1.9 fusion.56
  215.4 20.1 %reduce-scatter.11.cloned.1.call-done = f32[128,256]{0,1:T(8,128)} async-done(((f32[512,256]{0,1:T(8,128)}), f32[128,256]{0,1:T(8,128)}) %reduce-scatter.11.cloned.1.call-update) | async-done | bytes 131088 | tf_op jit(solution)/shard_map/reduce_scatter | solution.py:98
  238.2 4.6 all-to-all-start.5
  242.8 2.6 pad_maximum_fusion.2
  245.4 3.8 gather_fusion.10
  249.2 5.2 fusion.61
  254.4 4.7 gather_fusion.14
  259.1 3.4 multiply_reduce_fusion.1
  262.5 68.9 %all-gather.8 = f32[32,1,256]{2,1,0:T(1,128)S(1)} all-gather(f32[1,1,256]{2,1,0:T(1,128)S(1)} %bitcast.222), channel_id=5, replica_groups=mesh['row'=8,'col'=4] {'row','col'}, dimensions={0}, use_global_device_ids=true | all-gather | bytes 33792 | tf_op jit(solution)/shard_map/all_gather | solution.py:124
  331.4 2.3 fusion.47
  335.0 10.1 %all_to_all.62 = bf16[32,8,256]{2,1,0:T(8,128)(2,1)S(1)} all-to-all(bf16[32,8,256]{2,1,0:T(8,128)(2,1)S(1)} %bitcast.219), channel_id=1, replica_groups=mesh['row'=8,'col'=4] {'row','col'}, dimensions={0} | all-to-all | bytes 262144 | tf_op jit(solution)/shard_map/all_to_all | solution.py:88
  345.9 9.1 %all-gather.4 = bf16[1024,256]{1,0:T(8,128)(2,1)S(1)} all-gather(bf16[128,256]{1,0:T(8,128)(2,1)S(1)} %gather_fusion.17), channel_id=6, replica_groups=mesh['row'=8,'col'=4] {'row'}, dimensions={0}, use_global_device_ids=true | all-gather | bytes 589824 | tf_op jit(solution)/shard_map/all_gather | solution.py:97
  356.3 1.9 fusion.55
  361.3 20.1 %reduce-scatter.13.cloned.1.call-done = f32[128,256]{0,1:T(8,128)} async-done(((f32[512,256]{0,1:T(8,128)}), f32[128,256]{0,1:T(8,128)}) %reduce-scatter.13.cloned.1.call-update) | async-done | bytes 131088 | tf_op jit(solution)/shard_map/reduce_scatter | solution.py:98
  384.0 4.6 all-to-all-start.7
  388.7 2.6 pad_maximum_fusion.3
  391.3 3.8 gather_fusion.15
  395.1 5.1 fusion.62
  400.3 4.7 gather_fusion.19
  405.0 3.1 fusion.45
  409.3 14.0 %all_to_all.63 = bf16[32,8,256]{2,1,0:T(8,128)(2,1)S(1)} all-to-all(bf16[32,8,256]{2,1,0:T(8,128)(2,1)S(1)} %bitcast.220), channel_id=1, replica_groups=mesh['row'=8,'col'=4] {'row','col'}, dimensions={0} | all-to-all | bytes 262144 | tf_op jit(solution)/shard_map/all_to_all | solution.py:88
  424.1 9.1 %all-gather.5 = bf16[1024,256]{1,0:T(8,128)(2,1)S(1)} all-gather(bf16[128,256]{1,0:T(8,128)(2,1)S(1)} %gather_fusion.22), channel_id=7, replica_groups=mesh['row'=8,'col'=4] {'row'}, dimensions={0}, use_global_device_ids=true | all-gather | bytes 589824 | tf_op jit(solution)/shard_map/all_gather | solution.py:97
  434.6 1.9 fusion.54
  439.5 20.1 %reduce-scatter.15.cloned.1.call-done = f32[128,256]{0,1:T(8,128)} async-done(((f32[512,256]{0,1:T(8,128)}), f32[128,256]{0,1:T(8,128)}) %reduce-scatter.15.cloned.1.call-update) | async-done | bytes 131088 | tf_op jit(solution)/shard_map/reduce_scatter | solution.py:98
  462.3 4.6 all-to-all-start.9
  467.2 2.6 pad_maximum_fusion.4
  469.8 3.8 gather_fusion.20
  473.6 5.1 fusion.63
  478.8 4.7 gather_fusion.24
  483.4 3.4 fusion.43
  488.0 14.0 %all_to_all.64 = bf16[32,8,256]{2,1,0:T(8,128)(2,1)S(1)} all-to-all(bf16[32,8,256]{2,1,0:T(8,128)(2,1)S(1)} %bitcast.216), channel_id=1, replica_groups=mesh['row'=8,'col'=4] {'row','col'}, dimensions={0} | all-to-all | bytes 262144 | tf_op jit(solution)/shard_map/all_to_all | solution.py:88
  502.9 9.1 %all-gather.6 = bf16[1024,256]{1,0:T(8,128)(2,1)S(1)} all-gather(bf16[128,256]{1,0:T(8,128)(2,1)S(1)} %gather_fusion.27), channel_id=8, replica_groups=mesh['row'=8,'col'=4] {'row'}, dimensions={0}, use_global_device_ids=true | all-gather | bytes 589824 | tf_op jit(solution)/shard_map/all_gather | solution.py:97
  517.5 21.1 %reduce-scatter.17.cloned.1.call-done = f32[128,256]{0,1:T(8,128)} async-done(((f32[512,256]{0,1:T(8,128)}), f32[128,256]{0,1:T(8,128)}) %reduce-scatter.17.cloned.1.call-update) | async-done | bytes 131088 | tf_op jit(solution)/shard_map/reduce_scatter | solution.py:98
  541.3 4.3 all-to-all-start.11
  545.6 2.5 pad_maximum_fusion.5
  548.1 3.8 gather_fusion.25
  551.9 5.1 fusion.64
  557.0 4.7 gather_fusion.29
  561.7 2.5 multiply_reduce_fusion
  564.2 68.7 %all-gather.9 = f32[32,1,256]{2,1,0:T(1,128)S(1)} all-gather(f32[1,1,256]{2,1,0:T(1,128)S(1)} %bitcast.221), channel_id=9, replica_groups=mesh['row'=8,'col'=4] {'row','col'}, dimensions={0}, use_global_device_ids=true | all-gather | bytes 33792 | tf_op jit(solution)/shard_map/all_gather | solution.py:124
  (129 shorter events, 63.9 us)
Async XLA Ops:
  6.5 85.4 %copy-start = (f32[8,3,128,128]{3,2,1,0:T(8,128)S(1)}, f32[8,3,128,128]{3,2,1,0:T(8,128)}, u32[]{:S(2)}) copy-start(f32[8,3,128,128]{3,2,1,0:T(8,128)} %param.8) | copy-start | bytes 4718596
  26.3 17.1 %copy-start.2 = (s32[8,3]{0,1:T(4,128)S(1)}, s32[8,3]{0,1:T(4,128)}, u32[]{:S(2)}) copy-start(s32[8,3]{0,1:T(4,128)} %param.9) | copy-start | bytes 292
  26.4 32.3 %copy-start.1 = (bf16[512,1024]{1,0:T(8,128)(2,1)S(1)}, bf16[512,1024]{1,0:T(8,128)(2,1)}, u32[]{:S(2)}) copy-start(bf16[512,1024]{1,0:T(8,128)(2,1)} %param.11) | copy-start | bytes 3145732
  28.2 15.7 %all-to-all-start = ((bf16[32,8,256]{2,1,0:T(8,128)(2,1)}), bf16[32,8,256]{2,1,0:T(8,128)(2,1)S(1)}, u32[]{:S(2)}, u32[]{:S(2)}) async-start(bf16[32,8,256]{2,1,0:T(8,128)(2,1)} %bitcast.8), calls=%async_computation | async-start | bytes 262144 | tf_op jit(solution)/shard_map/all_to_all | solution.py:88
  35.5 44.4 %reduce-scatter.7.cloned.1.call-start = ((), (), s32[]{:S(2)}) async-start(), calls=%async_computation.18 | async-start | bytes 655360 | tf_op jit(solution)/shard_map/reduce_scatter | solution.py:98
  37.4 48.1 %collective-permute-start = (f32[256,256]{1,0:T(8,128)}, f32[256,256]{1,0:T(8,128)S(1)}, u32[]{:S(2)}, u32[]{:S(2)}) collective-permute-start(f32[256,256]{1,0:T(8,128)} %get-tuple-element.31), channel_id=1, source_target_pairs={{0,1},{1,2},{2,3},{3,4},{4,5},{5,6},{6,7},{7,8},{8,9},{9,10},{10,1... | collective-permute-start | bytes 786440 | tf_op jit(solution)/shard_map/ppermute | solution.py:15
  41.1 44.4 %collective-permute-start.1 = (f32[256,256]{1,0:T(8,128)}, f32[256,256]{1,0:T(8,128)}, u32[]{:S(2)}, u32[]{:S(2)}) collective-permute-start(f32[256,256]{1,0:T(8,128)} %get-tuple-element.32), channel_id=1, source_target_pairs={{1,0},{2,1},{3,2},{4,3},{5,4},{6,5},{7,6},{8,7},{9,8},{10,9},{11,1... | collective-permute-start | bytes 786440 | tf_op jit(solution)/shard_map/ppermute | solution.py:18
  44.8 15.4 %copy-start.3 = (s32[256]{0:T(256)S(1)}, s32[256]{0:T(256)}, u32[]{:S(2)}) copy-start(s32[256]{0:T(256)} %param.13) | copy-start | bytes 3076
  44.8 15.4 %copy-start.4 = (s32[256]{0:T(256)S(1)}, s32[256]{0:T(256)}, u32[]{:S(2)}) copy-start(s32[256]{0:T(256)} %param.12) | copy-start | bytes 3076
  82.6 14.5 %all-to-all-start.1 = ((f32[32,8,256]{2,1,0:T(8,128)}), f32[32,8,256]{2,1,0:T(8,128)S(1)}, u32[]{:S(2)}, u32[]{:S(2)}) async-start(f32[32,8,256]{2,1,0:T(8,128)} %bitcast.15), calls=%async_computation.2 | async-start | bytes 524288 | tf_op jit(solution)/shard_map/all_to_all | solution.py:101
  85.5 71.3 %reduce-scatter.9.cloned.1.call-start = ((), (), s32[]{:S(2)}) async-start(), calls=%async_computation.19 | async-start | bytes 655360 | tf_op jit(solution)/shard_map/reduce_scatter | solution.py:98
  133.6 30.5 %collective-permute-start.2 = (f32[256,256]{1,0:T(8,128)}, f32[256,256]{1,0:T(8,128)S(1)}, u32[]{:S(2)}, u32[]{:S(2)}) collective-permute-start(f32[256,256]{1,0:T(8,128)} %get-tuple-element.29), channel_id=1, source_target_pairs={{0,1},{1,2},{2,3},{3,4},{4,5},{5,6},{6,7},{7,8},{8,9},{9,10},{10,1... | collective-permute-start | bytes 786440 | tf_op jit(solution)/shard_map/ppermute | solution.py:15
  135.4 28.8 %collective-permute-start.3 = (f32[256,256]{1,0:T(8,128)}, f32[256,256]{1,0:T(8,128)}, u32[]{:S(2)}, u32[]{:S(2)}) collective-permute-start(f32[256,256]{1,0:T(8,128)} %get-tuple-element.30), channel_id=1, source_target_pairs={{1,0},{2,1},{3,2},{4,3},{5,4},{6,5},{7,6},{8,7},{9,8},{10,9},{11,1... | collective-permute-start | bytes 786440 | tf_op jit(solution)/shard_map/ppermute | solution.py:18
  159.5 16.3 %all-to-all-start.3 = ((f32[32,8,256]{2,1,0:T(8,128)}), f32[32,8,256]{2,1,0:T(8,128)S(1)}, u32[]{:S(2)}, u32[]{:S(2)}) async-start(f32[32,8,256]{2,1,0:T(8,128)} %bitcast.27), calls=%async_computation.5 | async-start | bytes 524288 | tf_op jit(solution)/shard_map/all_to_all | solution.py:101
  164.1 71.3 %reduce-scatter.11.cloned.1.call-start = ((), (), s32[]{:S(2)}) async-start(), calls=%async_computation.20 | async-start | bytes 655360 | tf_op jit(solution)/shard_map/reduce_scatter | solution.py:98
  212.3 30.5 %collective-permute-start.4 = (f32[256,256]{1,0:T(8,128)}, f32[256,256]{1,0:T(8,128)S(1)}, u32[]{:S(2)}, u32[]{:S(2)}) collective-permute-start(f32[256,256]{1,0:T(8,128)} %get-tuple-element.27), channel_id=1, source_target_pairs={{0,1},{1,2},{2,3},{3,4},{4,5},{5,6},{6,7},{7,8},{8,9},{9,10},{10,1... | collective-permute-start | bytes 786440 | tf_op jit(solution)/shard_map/ppermute | solution.py:15
  214.1 28.7 %collective-permute-start.5 = (f32[256,256]{1,0:T(8,128)}, f32[256,256]{1,0:T(8,128)}, u32[]{:S(2)}, u32[]{:S(2)}) collective-permute-start(f32[256,256]{1,0:T(8,128)} %get-tuple-element.28), channel_id=1, source_target_pairs={{1,0},{2,1},{3,2},{4,3},{5,4},{6,5},{7,6},{8,7},{9,8},{10,9},{11,1... | collective-permute-start | bytes 786440 | tf_op jit(solution)/shard_map/ppermute | solution.py:18
  238.2 16.2 %all-to-all-start.5 = ((f32[32,8,256]{2,1,0:T(8,128)}), f32[32,8,256]{2,1,0:T(8,128)S(1)}, u32[]{:S(2)}, u32[]{:S(2)}) async-start(f32[32,8,256]{2,1,0:T(8,128)} %bitcast.38), calls=%async_computation.8 | async-start | bytes 524288 | tf_op jit(solution)/shard_map/all_to_all | solution.py:101
  242.8 138.6 %reduce-scatter.13.cloned.1.call-start = ((), (), s32[]{:S(2)}) async-start(), calls=%async_computation.21 | async-start | bytes 655360 | tf_op jit(solution)/shard_map/reduce_scatter | solution.py:98
  358.2 30.5 %collective-permute-start.6 = (f32[256,256]{1,0:T(8,128)}, f32[256,256]{1,0:T(8,128)S(1)}, u32[]{:S(2)}, u32[]{:S(2)}) collective-permute-start(f32[256,256]{1,0:T(8,128)} %get-tuple-element.25), channel_id=1, source_target_pairs={{0,1},{1,2},{2,3},{3,4},{4,5},{5,6},{6,7},{7,8},{8,9},{9,10},{10,1... | collective-permute-start | bytes 786440 | tf_op jit(solution)/shard_map/ppermute | solution.py:15
  360.0 28.7 %collective-permute-start.7 = (f32[256,256]{1,0:T(8,128)}, f32[256,256]{1,0:T(8,128)}, u32[]{:S(2)}, u32[]{:S(2)}) collective-permute-start(f32[256,256]{1,0:T(8,128)} %get-tuple-element.26), channel_id=1, source_target_pairs={{1,0},{2,1},{3,2},{4,3},{5,4},{6,5},{7,6},{8,7},{9,8},{10,9},{11,1... | collective-permute-start | bytes 786440 | tf_op jit(solution)/shard_map/ppermute | solution.py:18
  384.0 16.2 %all-to-all-start.7 = ((f32[32,8,256]{2,1,0:T(8,128)}), f32[32,8,256]{2,1,0:T(8,128)S(1)}, u32[]{:S(2)}, u32[]{:S(2)}) async-start(f32[32,8,256]{2,1,0:T(8,128)} %bitcast.50), calls=%async_computation.11 | async-start | bytes 524288 | tf_op jit(solution)/shard_map/all_to_all | solution.py:101
  388.7 71.0 %reduce-scatter.15.cloned.1.call-start = ((), (), s32[]{:S(2)}) async-start(), calls=%async_computation.22 | async-start | bytes 655360 | tf_op jit(solution)/shard_map/reduce_scatter | solution.py:98
  436.5 30.7 %collective-permute-start.8 = (f32[256,256]{1,0:T(8,128)}, f32[256,256]{1,0:T(8,128)S(1)}, u32[]{:S(2)}, u32[]{:S(2)}) collective-permute-start(f32[256,256]{1,0:T(8,128)} %get-tuple-element.23), channel_id=1, source_target_pairs={{0,1},{1,2},{2,3},{3,4},{4,5},{5,6},{6,7},{7,8},{8,9},{9,10},{10,1... | collective-permute-start | bytes 786440 | tf_op jit(solution)/shard_map/ppermute | solution.py:15
  438.2 29.0 %collective-permute-start.9 = (f32[256,256]{1,0:T(8,128)}, f32[256,256]{1,0:T(8,128)}, u32[]{:S(2)}, u32[]{:S(2)}) collective-permute-start(f32[256,256]{1,0:T(8,128)} %get-tuple-element.24), channel_id=1, source_target_pairs={{1,0},{2,1},{3,2},{4,3},{5,4},{6,5},{7,6},{8,7},{9,8},{10,9},{11,1... | collective-permute-start | bytes 786440 | tf_op jit(solution)/shard_map/ppermute | solution.py:18
  462.3 16.4 %all-to-all-start.9 = ((f32[32,8,256]{2,1,0:T(8,128)}), f32[32,8,256]{2,1,0:T(8,128)S(1)}, u32[]{:S(2)}, u32[]{:S(2)}) async-start(f32[32,8,256]{2,1,0:T(8,128)} %bitcast.61), calls=%async_computation.14 | async-start | bytes 524288 | tf_op jit(solution)/shard_map/all_to_all | solution.py:101
  466.9 71.7 %reduce-scatter.17.cloned.1.call-start = ((), (), s32[]{:S(2)}) async-start(), calls=%async_computation.23 | async-start | bytes 655360 | tf_op jit(solution)/shard_map/reduce_scatter | solution.py:98
  514.4 31.1 %collective-permute-start.10 = (f32[256,256]{1,0:T(8,128)S(1)}, f32[256,256]{1,0:T(8,128)S(1)}, u32[]{:S(2)}, u32[]{:S(2)}) collective-permute-start(f32[256,256]{1,0:T(8,128)S(1)} %get-tuple-element.21), channel_id=1, source_target_pairs={{0,1},{1,2},{2,3},{3,4},{4,5},{5,6},{6,7},{7,8},{8,9},{9,10},{10,1... | collective-permute-start | bytes 786440 | tf_op jit(solution)/shard_map/ppermute | solution.py:15
  516.2 29.4 %collective-permute-start.11 = (f32[256,256]{1,0:T(8,128)S(1)}, f32[256,256]{1,0:T(8,128)S(1)}, u32[]{:S(2)}, u32[]{:S(2)}) collective-permute-start(f32[256,256]{1,0:T(8,128)S(1)} %get-tuple-element.22), channel_id=1, source_target_pairs={{1,0},{2,1},{3,2},{4,3},{5,4},{6,5},{7,6},{8,7},{9,8},{10,9},{11,1... | collective-permute-start | bytes 786440 | tf_op jit(solution)/shard_map/ppermute | solution.py:18
  541.3 15.7 %all-to-all-start.11 = ((f32[32,8,256]{2,1,0:T(8,128)}), f32[32,8,256]{2,1,0:T(8,128)S(1)}, u32[]{:S(2)}, u32[]{:S(2)}) async-start(f32[32,8,256]{2,1,0:T(8,128)} %bitcast.72), calls=%async_computation.17 | async-start | bytes 524288 | tf_op jit(solution)/shard_map/all_to_all | solution.py:101
Sparse Core Ops, SparseCore 0:
  60.1 19.7 reduce-scatter.6
  131.9 24.8 reduce-scatter.8
  210.5 24.8 reduce-scatter.10
  356.4 24.8 reduce-scatter.12
  434.7 24.8 reduce-scatter.14
  513.5 25.0 reduce-scatter.16
